TPU v7x, 256 devices: a whole 4x4x8 slice. The times are simulated.
256 devices in a mesh: row: 16 (over z, core), col: 16 (over y, x).
Axes of the slice: x: 4, y: 4, z: 8, core: 2. Of those that a mesh axis runs over, the one named last changes fastest.
Arguments:
- matrix: float32 [8192, 8192], P('row', 'col'), as said below
Outputs:
- reduced: float32 [8192, 8192], P('row', 'col')
Inputs may be any that keep to these rules, and one draw needn't show every extreme that they name: matrix is symmetric.
All inputs are finite; a program needn't handle non-finite values.
Results may differ from a plain program's by a relative error of at most 0.00014.
Values sent between devices are 32-bit elements; how exact they have to be, the bound alone decides.
A program may use at most 64 MiB of HBM per device.

v0:
```python
import jax
import jax.numpy as jnp
from jax import lax
from jax.sharding import PartitionSpec as P

BLOCK = 256
PANELS = 2
HIGH = lax.Precision.HIGHEST


def broadcast(block, axis, source):
    block = jnp.where(lax.axis_index(axis) == source, block, jnp.zeros_like(block))
    return lax.psum(block, axis)


def mult(left, right):
    return jnp.dot(left, right, precision=HIGH, preferred_element_type=jnp.float32)


def inverse_transposed(shifted):
    factor = jnp.linalg.cholesky(mult(shifted, shifted.T))
    half = jax.scipy.linalg.solve_triangular(factor, shifted, lower=True)
    return jax.scipy.linalg.solve_triangular(factor, half, lower=True, trans="T")


def reflector_columns(local_rows, column, ratio):
    pieces = broadcast(local_rows, "row", column * ratio + 0)
    return pieces


def update_columns(local_rows, column, ratio):
    pieces = broadcast(local_rows, "row", column * ratio + 0)
    return pieces


def reflect(current, index, row_index, column, ratio):
    height = current.shape[0]
    lead = (index + 1) * BLOCK
    owner = lead // height
    offset_top = lead - owner * height
    rows = row_index * height + jnp.arange(height, dtype=jnp.int32)
    local_panel = jnp.where(
        (rows >= lead)[:, None], current[:, index * BLOCK : (index + 1) * BLOCK], jnp.float32(0.0)
    )
    panel = broadcast(local_panel, "col", 0)
    local_gram = mult(panel.T, panel)
    gram = lax.psum(local_gram, "row")
    top_panel = broadcast(panel[offset_top : offset_top + BLOCK], "row", owner)
    lower = jnp.linalg.cholesky(gram)
    basis = jax.scipy.linalg.solve_triangular(lower, panel.T, lower=True).T
    top = jax.scipy.linalg.solve_triangular(lower, top_panel.T, lower=True).T
    kernel = inverse_transposed(jnp.eye(BLOCK, dtype=jnp.float32) + top)
    unit = ((rows - lead)[:, None] == jnp.arange(BLOCK, dtype=jnp.int32)[None, :]).astype(
        jnp.float32
    )
    vectors = basis + unit
    vectors_cols = reflector_columns(vectors, column, ratio)
    product = lax.psum(mult(current, vectors_cols), "col")
    inner = lax.psum(mult(vectors.T, product), "row")
    coupled = mult(kernel.T, mult(inner, kernel))
    update = mult(product, kernel) - 0.5 * mult(vectors, coupled)
    update_cols = update_columns(update, column, ratio)
    return current - mult(update, vectors_cols.T) - mult(vectors, update_cols.T)


def per_device(matrix):
    row_index = lax.axis_index("row")
    column = lax.axis_index("col")
    ratio = lax.axis_size("row") // lax.axis_size("col")
    current = matrix
    for index in range(PANELS):
        current = reflect(current, index, row_index, column, ratio)
    return current


def solution(mesh):
    in_specs = (P("row", "col"),)
    out_specs = P("row", "col")
    return jax.shard_map(
        per_device, mesh=mesh, in_specs=in_specs, out_specs=out_specs, check_vma=False
    )
```

profile of v0, /device:TPU:1, one launch (start us, length us, event | category | flops | bytes accessed | tf_op | source)
XLA Modules:
  0.0 1581.3 jit_solution(13761343751059832308)
XLA Ops:
  9.0 99.1 %all-reduce.16.cloned.1.call-done = f32[512,256]{0,1:T(8,128)} async-done(((f32[512,256]{0,1:T(8,128)}), f32[512,256]{0,1:T(8,128)}) %all-reduce.16.cloned.1.call-update) | async-done | bytes 524304 | tf_op jit(solution)/shard_map/psum | solution.py:13
  110.8 111.6 %all-reduce.18.cloned.1.call-done = f32[256,256]{0,1:T(8,128)} async-done(((f32[256,256]{0,1:T(8,128)}), f32[256,256]{0,1:T(8,128)}) %all-reduce.18.cloned.1.call-update) | async-done | bytes 262160 | tf_op jit(solution)/shard_map/psum | solution.py:47
  223.6 11.7 cholesky.214
  245.6 11.7 cholesky.231
  263.9 19.7 %custom-call.26 = f32[2,128,128]{1,2,0:T(8,128)S(1)} custom-call(f32[2,128,128]{2,1,0:T(8,128)S(1)} %get-tuple-element.63), custom_call_target="InvertDiagBlocksLowerTriangular" | custom-call | tf_op jit(solution)/shard_map/jit(_solve_triangular)/triangular_solve | solution.py:50
  285.8 111.3 %all-reduce.20.cloned.1.call-done = f32[512,256]{0,1:T(8,128)} async-done(((f32[512,256]{0,1:T(8,128)}), f32[512,256]{0,1:T(8,128)}) %all-reduce.20.cloned.1.call-update) | async-done | bytes 524304 | tf_op jit(solution)/shard_map/psum | solution.py:13
  400.8 93.6 %all-reduce.22.cloned.1.call-done = f32[512,256]{0,1:T(8,128)} async-done(((f32[512,256]{0,1:T(8,128)}), f32[512,256]{0,1:T(8,128)}) %all-reduce.22.cloned.1.call-update) | async-done | bytes 524304 | tf_op jit(solution)/shard_map/psum | solution.py:58
  496.8 112.6 %all-reduce.38.cloned.1.call-done = (f32[256,256]{1,0:T(8,128)}, f32[256,256]{1,0:T(8,128)}) async-done(((f32[256,256]{1,0:T(8,128)}, f32[256,256]{1,0:T(8,128)}), (f32[256,256]{1,0:T(8,128)}, f32[256,256]{1,0:T(8,128)})) %all-reduce.38.cloned.1.call-update) | async-done | bytes 524304 | tf_op jit(solution)/shard_map/psum | solution.py:13
  612.2 11.7 cholesky.248
  634.3 11.7 cholesky.265
  653.0 19.7 %custom-call.30 = f32[2,128,128]{1,2,0:T(8,128)S(1)} custom-call(f32[2,128,128]{2,1,0:T(8,128)S(1)} %get-tuple-element.66), custom_call_target="InvertDiagBlocksLowerTriangular" | custom-call | tf_op jit(solution)/shard_map/jit(_solve_triangular)/triangular_solve | solution.py:23
  682.2 108.2 %all-reduce.24.cloned.1.call-done = f32[512,256]{0,1:T(8,128)} async-done(((f32[512,256]{0,1:T(8,128)}), f32[512,256]{0,1:T(8,128)}) %all-reduce.24.cloned.1.call-update) | async-done | bytes 524304 | tf_op jit(solution)/shard_map/psum | solution.py:13
  793.5 94.3 %all-reduce.26.cloned.1.call-done = f32[512,256]{0,1:T(8,128)} async-done(((f32[512,256]{0,1:T(8,128)}), f32[512,256]{0,1:T(8,128)}) %all-reduce.26.cloned.1.call-update) | async-done | bytes 524304 | tf_op jit(solution)/shard_map/psum | solution.py:13
  890.6 111.4 %all-reduce.28.cloned.1.call-done = f32[256,256]{0,1:T(8,128)} async-done(((f32[256,256]{0,1:T(8,128)}), f32[256,256]{0,1:T(8,128)}) %all-reduce.28.cloned.1.call-update) | async-done | bytes 262160 | tf_op jit(solution)/shard_map/psum | solution.py:47
  1003.3 11.7 cholesky.282
  1025.3 11.7 cholesky.299
  1044.0 19.7 %custom-call.32 = f32[2,128,128]{1,2,0:T(8,128)S(1)} custom-call(f32[2,128,128]{2,1,0:T(8,128)S(1)} %get-tuple-element.67), custom_call_target="InvertDiagBlocksLowerTriangular" | custom-call | tf_op jit(solution)/shard_map/jit(_solve_triangular)/triangular_solve | solution.py:50
  1065.9 111.3 %all-reduce.30.cloned.1.call-done = f32[512,256]{0,1:T(8,128)} async-done(((f32[512,256]{0,1:T(8,128)}), f32[512,256]{0,1:T(8,128)}) %all-reduce.30.cloned.1.call-update) | async-done | bytes 524304 | tf_op jit(solution)/shard_map/psum | solution.py:13
  1181.6 93.6 %all-reduce.32.cloned.1.call-done = f32[512,256]{1,0:T(8,128)} async-done(((f32[512,256]{1,0:T(8,128)}), f32[512,256]{1,0:T(8,128)}) %all-reduce.32.cloned.1.call-update) | async-done | bytes 524304 | tf_op jit(solution)/shard_map/psum | solution.py:58
  1278.0 112.2 %all-reduce.36.cloned.1.call-done = (f32[256,256]{1,0:T(8,128)}, f32[256,256]{1,0:T(8,128)}) async-done(((f32[256,256]{1,0:T(8,128)}, f32[256,256]{1,0:T(8,128)}), (f32[256,256]{1,0:T(8,128)}, f32[256,256]{1,0:T(8,128)})) %all-reduce.36.cloned.1.call-update) | async-done | bytes 524304 | tf_op jit(solution)/shard_map/psum | solution.py:13
  1393.0 11.7 cholesky.316
  1415.1 11.7 cholesky.333
  1433.6 19.7 %custom-call.36 = f32[2,128,128]{1,2,0:T(8,128)S(1)} custom-call(f32[2,128,128]{2,1,0:T(8,128)S(1)} %get-tuple-element.70), custom_call_target="InvertDiagBlocksLowerTriangular" | custom-call | tf_op jit(solution)/shard_map/jit(_solve_triangular)/triangular_solve | solution.py:23
  1462.8 108.0 %all-reduce.34.cloned.1.call-done = f32[512,256]{0,1:T(8,128)} async-done(((f32[512,256]{0,1:T(8,128)}), f32[512,256]{0,1:T(8,128)}) %all-reduce.34.cloned.1.call-update) | async-done | bytes 524304 | tf_op jit(solution)/shard_map/psum | solution.py:13
  (189 shorter events, 137.9 us)
Async XLA Ops:
  6.5 101.6 %all-reduce.16.cloned.1.call-start = ((), (), s32[]{:S(2)}) async-start(), calls=%async_computation | async-start | bytes 1048576 | tf_op jit(solution)/shard_map/psum | solution.py:13
  9.0 213.3 %all-reduce.18.cloned.1.call-start = ((), (), s32[]{:S(2)}) async-start(), calls=%async_computation.1 | async-start | bytes 524288 | tf_op jit(solution)/shard_map/psum | solution.py:47
  110.7 286.4 %all-reduce.20.cloned.1.call-start = ((), (), s32[]{:S(2)}) async-start(), calls=%async_computation.2 | async-start | bytes 1048576 | tf_op jit(solution)/shard_map/psum | solution.py:13
  222.3 1.2 copy-start.7
  259.5 24.1 %copy-start = (f32[512,256]{0,1:T(8,128)S(1)}, f32[512,256]{0,1:T(8,128)}, u32[]{:S(2)}) copy-start(f32[512,256]{0,1:T(8,128)} %all-reduce.16.cloned.1.call-done) | copy-start | bytes 1572868
  284.4 112.7 %copy-start.2 = (f32[512,512]{1,0:T(8,128)S(1)}, f32[512,512]{1,0:T(8,128)}, u32[]{:S(2)}) copy-start(f32[512,512]{1,0:T(8,128)} %param.8) | copy-start | bytes 3145732
  285.7 208.6 %all-reduce.22.cloned.1.call-start = ((), (), s32[]{:S(2)}) async-start(), calls=%async_computation.3 | async-start | bytes 1048576 | tf_op jit(solution)/shard_map/psum | solution.py:58
  400.0 209.5 %all-reduce.38.cloned.1.call-start = ((), (), s32[]{:S(2)}) async-start(), calls=%async_computation.11 | async-start | bytes 1048576 | tf_op jit(solution)/shard_map/psum | solution.py:13
  496.8 293.6 %all-reduce.24.cloned.1.call-start = ((), (), s32[]{:S(2)}) async-start(), calls=%async_computation.4 | async-start | bytes 1048576 | tf_op jit(solution)/shard_map/psum | solution.py:13
  609.5 1.3 copy-start.11
  674.3 1.0 copy-start.10
  675.7 1.0 copy-start.4
  679.1 1.0 copy-start.6
  679.1 208.7 %all-reduce.26.cloned.1.call-start = ((), (), s32[]{:S(2)}) async-start(), calls=%async_computation.5 | async-start | bytes 1048576 | tf_op jit(solution)/shard_map/psum | solution.py:13
  793.5 208.6 %all-reduce.28.cloned.1.call-start = ((), (), s32[]{:S(2)}) async-start(), calls=%async_computation.6 | async-start | bytes 524288 | tf_op jit(solution)/shard_map/psum | solution.py:47
  890.4 286.7 %all-reduce.30.cloned.1.call-start = ((), (), s32[]{:S(2)}) async-start(), calls=%async_computation.7 | async-start | bytes 1048576 | tf_op jit(solution)/shard_map/psum | solution.py:13
  1002.0 1.2 copy-start.8
  1039.8 23.9 %copy-start.1 = (f32[512,256]{0,1:T(8,128)S(1)}, f32[512,256]{0,1:T(8,128)}, u32[]{:S(2)}) copy-start(f32[512,256]{0,1:T(8,128)} %all-reduce.26.cloned.1.call-done) | copy-start | bytes 1572868
  1065.8 209.4 %all-reduce.32.cloned.1.call-start = ((), (), s32[]{:S(2)}) async-start(), calls=%async_computation.8 | async-start | bytes 1048576 | tf_op jit(solution)/shard_map/psum | solution.py:58
  1180.8 209.5 %all-reduce.36.cloned.1.call-start = ((), (), s32[]{:S(2)}) async-start(), calls=%async_computation.10 | async-start | bytes 1048576 | tf_op jit(solution)/shard_map/psum | solution.py:13
  1277.6 293.3 %all-reduce.34.cloned.1.call-start = ((), (), s32[]{:S(2)}) async-start(), calls=%async_computation.9 | async-start | bytes 1048576 | tf_op jit(solution)/shard_map/psum | solution.py:13
  1390.3 1.3 copy-start.12
  1456.3 1.0 copy-start.3
  1459.7 1.0 copy-start.5
  (1 other events, 1.0 us)
Sparse Core Ops, SparseCore 0:
  10.5 97.5 all-reduce.15
  110.8 111.4 all-reduce.17
  285.8 111.1 all-reduce.19
  400.1 94.1 all-reduce.21
  496.9 112.5 all-reduce.37
  679.2 111.1 all-reduce.23
  793.6 94.1 all-reduce.25
  890.5 111.4 all-reduce.27
  1065.9 111.1 all-reduce.29
  1180.9 94.1 all-reduce.31
  1277.7 112.5 all-reduce.35
  1459.8 110.9 all-reduce.33
where the time goes:
time: 1590 us; the launch traced here: 1580 us
  waiting for transfers between devices  1270 us (80%)
  other arithmetic  222 us (14%)
  matrix products  44.4 us (3%)
  local copies, waits for them, and re-layouts  25.8 us (2%)
  between operations  19.8 us (1%)
    psum x8, waiting for transfers between devices, broadcast(): return lax.psum(block, axis)  857 us
    psum x2, waiting for transfers between devices, reflect(): gram = lax.psum(local_gram, 'row')  223 us
    psum x2, waiting for transfers between devices, reflect(): product = lax.psum(mult(current, vectors_cols), 'col')  187 us
    another operation x14, other arithmetic, inverse_transposed(): factor = jnp.linalg.cholesky(mult(shifted, shifted.T))  69.2 us
    another operation x13, other arithmetic, reflect(): lower = jnp.linalg.cholesky(gram)  68.7 us
    another operation x5, other arithmetic, reflect(): basis = jax.scipy.linalg.solve_triangular(lower, panel.T, lower=True).T  39.4 us
    another operation x4, other arithmetic, inverse_transposed(): jax.scipy.linalg.solve_triangular(factor, half, lower=True, trans='T')  39.4 us
    dot_general x20, matrix products, mult(): jnp.dot(left, right, precision=HIGH, preferred_element_type=jnp.float32)  32.7 us
  transfers between devices with their start and end apart: 12, of which 12 were waited for; matrix products, arithmetic and copies ran while one was open for 0% of the time, Pallas kernels for 0%

commit v1 on v0

--- a/solution.py
+++ b/solution.py
@@ -44,7 +44,8 @@
     )
     panel = broadcast(local_panel, "col", 0)
     local_gram = mult(panel.T, panel)
-    gram = lax.psum(local_gram, "row")
+    terms = lax.all_gather(local_gram, "row")
+    gram = jnp.sum(terms, axis=0)
     top_panel = broadcast(panel[offset_top : offset_top + BLOCK], "row", owner)
     lower = jnp.linalg.cholesky(gram)
     basis = jax.scipy.linalg.solve_triangular(lower, panel.T, lower=True).T

time: 1590 us -> 1460 us (0.918)
  waiting for transfers between devices: 1270 us -> 1130 us
    psum x2 -> x0, waiting for transfers between devices: 223 us -> none  [reflect(): gram = lax.psum(local_gram, 'row')]
    all_gather x0 -> x2, waiting for transfers between devices: none -> 87.3 us  [reflect(): terms = lax.all_gather(local_gram, 'row')]
where the time goes in v1:
time: 1460 us; the launch traced here: 1450 us
  waiting for transfers between devices  1130 us (77%)
  other arithmetic  227 us (16%)
  matrix products  48 us (3%)
  between operations  20 us (1%)
  local copies, waits for them, and re-layouts  19.6 us (1%)
    psum x8, waiting for transfers between devices, broadcast(): return lax.psum(block, axis)  855 us
    psum x2, waiting for transfers between devices, reflect(): product = lax.psum(mult(current, vectors_cols), 'col')  187 us
    all_gather x2, waiting for transfers between devices, reflect(): terms = lax.all_gather(local_gram, 'row')  87.3 us
    another operation x14, other arithmetic, inverse_transposed(): factor = jnp.linalg.cholesky(mult(shifted, shifted.T))  69.2 us
    another operation x13, other arithmetic, reflect(): lower = jnp.linalg.cholesky(gram)  68.7 us
    another operation x5, other arithmetic, reflect(): basis = jax.scipy.linalg.solve_triangular(lower, panel.T, lower=True).T  39.4 us
    another operation x4, other arithmetic, inverse_transposed(): jax.scipy.linalg.solve_triangular(factor, half, lower=True, trans='T')  39.4 us
    dot_general x20, matrix products, mult(): jnp.dot(left, right, precision=HIGH, preferred_element_type=jnp.float32)  34.7 us
  transfers between devices with their start and end apart: 12, of which 12 were waited for; matrix products, arithmetic and copies ran while one was open for 0% of the time, Pallas kernels for 0%

profile of v1, /device:TPU:1, one launch (start us, length us, event | category | flops | bytes accessed | tf_op | source)
XLA Modules:
  0.0 1446.0 jit_solution(5462608233593649379)
XLA Ops:
  9.0 99.1 %all-reduce.14.cloned.1.call-done = f32[512,256]{0,1:T(8,128)} async-done(((f32[512,256]{0,1:T(8,128)}), f32[512,256]{0,1:T(8,128)}) %all-reduce.14.cloned.1.call-update) | async-done | bytes 524304 | tf_op jit(solution)/shard_map/psum | solution.py:13
  110.8 43.8 %all-gather.5.cloned.1.call-done = f32[4096,256]{1,0:T(8,128)} async-done(((f32[256,256]{1,0:T(8,128)}), f32[4096,256]{1,0:T(8,128)}) %all-gather.5.cloned.1.call-update) | async-done | bytes 4194320 | tf_op jit(solution)/shard_map/all_gather | solution.py:47
  157.4 11.7 cholesky.214
  179.4 11.7 cholesky.231
  197.8 19.7 %custom-call.26 = f32[2,128,128]{1,2,0:T(8,128)S(1)} custom-call(f32[2,128,128]{2,1,0:T(8,128)S(1)} %get-tuple-element.63), custom_call_target="InvertDiagBlocksLowerTriangular" | custom-call | tf_op jit(solution)/shard_map/jit(_solve_triangular)/triangular_solve | solution.py:51
  219.7 108.8 %all-reduce.16.cloned.1.call-done = f32[512,256]{0,1:T(8,128)} async-done(((f32[512,256]{0,1:T(8,128)}), f32[512,256]{0,1:T(8,128)}) %all-reduce.16.cloned.1.call-update) | async-done | bytes 524304 | tf_op jit(solution)/shard_map/psum | solution.py:13
  332.2 93.6 %all-reduce.18.cloned.1.call-done = f32[512,256]{0,1:T(8,128)} async-done(((f32[512,256]{0,1:T(8,128)}), f32[512,256]{0,1:T(8,128)}) %all-reduce.18.cloned.1.call-update) | async-done | bytes 524304 | tf_op jit(solution)/shard_map/psum | solution.py:59
  428.3 112.6 %all-reduce.32.cloned.1.call-done = (f32[256,256]{1,0:T(8,128)}, f32[256,256]{1,0:T(8,128)}) async-done(((f32[256,256]{1,0:T(8,128)}, f32[256,256]{1,0:T(8,128)}), (f32[256,256]{1,0:T(8,128)}, f32[256,256]{1,0:T(8,128)})) %all-reduce.32.cloned.1.call-update) | async-done | bytes 524304 | tf_op jit(solution)/shard_map/psum | solution.py:13
  544.5 11.7 cholesky.248
  566.6 11.7 cholesky.265
  585.1 19.7 %custom-call.30 = f32[2,128,128]{1,2,0:T(8,128)S(1)} custom-call(f32[2,128,128]{2,1,0:T(8,128)S(1)} %get-tuple-element.66), custom_call_target="InvertDiagBlocksLowerTriangular" | custom-call | tf_op jit(solution)/shard_map/jit(_solve_triangular)/triangular_solve | solution.py:23
  613.2 109.1 %all-reduce.20.cloned.1.call-done = f32[512,256]{0,1:T(8,128)} async-done(((f32[512,256]{0,1:T(8,128)}), f32[512,256]{0,1:T(8,128)}) %all-reduce.20.cloned.1.call-update) | async-done | bytes 524304 | tf_op jit(solution)/shard_map/psum | solution.py:13
  725.5 94.3 %all-reduce.22.cloned.1.call-done = f32[512,256]{0,1:T(8,128)} async-done(((f32[512,256]{0,1:T(8,128)}), f32[512,256]{0,1:T(8,128)}) %all-reduce.22.cloned.1.call-update) | async-done | bytes 524304 | tf_op jit(solution)/shard_map/psum | solution.py:13
  822.8 43.4 %all-gather.7.cloned.1.call-done = f32[4096,256]{1,0:T(8,128)} async-done(((f32[256,256]{1,0:T(8,128)}), f32[4096,256]{1,0:T(8,128)}) %all-gather.7.cloned.1.call-update) | async-done | bytes 4194320 | tf_op jit(solution)/shard_map/all_gather | solution.py:47
  869.0 11.7 cholesky.282
  891.1 11.7 cholesky.299
  909.8 19.7 %custom-call.32 = f32[2,128,128]{1,2,0:T(8,128)S(1)} custom-call(f32[2,128,128]{2,1,0:T(8,128)S(1)} %get-tuple-element.67), custom_call_target="InvertDiagBlocksLowerTriangular" | custom-call | tf_op jit(solution)/shard_map/jit(_solve_triangular)/triangular_solve | solution.py:51
  931.7 109.0 %all-reduce.24.cloned.1.call-done = f32[512,256]{0,1:T(8,128)} async-done(((f32[512,256]{0,1:T(8,128)}), f32[512,256]{0,1:T(8,128)}) %all-reduce.24.cloned.1.call-update) | async-done | bytes 524304 | tf_op jit(solution)/shard_map/psum | solution.py:13
  1045.2 93.6 %all-reduce.26.cloned.1.call-done = f32[512,256]{1,0:T(8,128)} async-done(((f32[512,256]{1,0:T(8,128)}), f32[512,256]{1,0:T(8,128)}) %all-reduce.26.cloned.1.call-update) | async-done | bytes 524304 | tf_op jit(solution)/shard_map/psum | solution.py:59
  1141.2 112.6 %all-reduce.30.cloned.1.call-done = (f32[256,256]{1,0:T(8,128)}, f32[256,256]{1,0:T(8,128)}) async-done(((f32[256,256]{1,0:T(8,128)}, f32[256,256]{1,0:T(8,128)}), (f32[256,256]{1,0:T(8,128)}, f32[256,256]{1,0:T(8,128)})) %all-reduce.30.cloned.1.call-update) | async-done | bytes 524304 | tf_op jit(solution)/shard_map/psum | solution.py:13
  1257.4 11.7 cholesky.316
  1279.5 11.7 cholesky.333
  1298.1 19.7 %custom-call.36 = f32[2,128,128]{1,2,0:T(8,128)S(1)} custom-call(f32[2,128,128]{2,1,0:T(8,128)S(1)} %get-tuple-element.70), custom_call_target="InvertDiagBlocksLowerTriangular" | custom-call | tf_op jit(solution)/shard_map/jit(_solve_triangular)/triangular_solve | solution.py:23
  1326.1 109.2 %all-reduce.28.cloned.1.call-done = f32[512,256]{0,1:T(8,128)} async-done(((f32[512,256]{0,1:T(8,128)}), f32[512,256]{0,1:T(8,128)}) %all-reduce.28.cloned.1.call-update) | async-done | bytes 524304 | tf_op jit(solution)/shard_map/psum | solution.py:13
  (179 shorter events, 140.2 us)
Async XLA Ops:
  6.5 101.6 %all-reduce.14.cloned.1.call-start = ((), (), s32[]{:S(2)}) async-start(), calls=%async_computation | async-start | bytes 1048576 | tf_op jit(solution)/shard_map/psum | solution.py:13
  9.0 145.6 %all-gather.5.cloned.1.call-start = ((), (), s32[]{:S(2)}) async-start(), calls=%async_computation.8 | async-start | bytes 4456448 | tf_op jit(solution)/shard_map/all_gather | solution.py:47
  110.7 217.8 %all-reduce.16.cloned.1.call-start = ((), (), s32[]{:S(2)}) async-start(), calls=%async_computation.1 | async-start | bytes 1048576 | tf_op jit(solution)/shard_map/psum | solution.py:13
  154.6 62.9 %copy-start = (f32[512,256]{0,1:T(8,128)S(1)}, f32[512,256]{0,1:T(8,128)}, u32[]{:S(2)}) copy-start(f32[512,256]{0,1:T(8,128)} %all-reduce.14.cloned.1.call-done) | copy-start | bytes 1572868
  157.1 171.4 %copy-start.2 = (f32[512,512]{1,0:T(8,128)S(1)}, f32[512,512]{1,0:T(8,128)}, u32[]{:S(2)}) copy-start(f32[512,512]{1,0:T(8,128)} %param.8) | copy-start | bytes 3145732
  219.7 206.2 %all-reduce.18.cloned.1.call-start = ((), (), s32[]{:S(2)}) async-start(), calls=%async_computation.2 | async-start | bytes 1048576 | tf_op jit(solution)/shard_map/psum | solution.py:59
  331.4 209.5 %all-reduce.32.cloned.1.call-start = ((), (), s32[]{:S(2)}) async-start(), calls=%async_computation.11 | async-start | bytes 1048576 | tf_op jit(solution)/shard_map/psum | solution.py:13
  428.2 294.1 %all-reduce.20.cloned.1.call-start = ((), (), s32[]{:S(2)}) async-start(), calls=%async_computation.3 | async-start | bytes 1048576 | tf_op jit(solution)/shard_map/psum | solution.py:13
  544.2 64.4 %copy-start.4 = (f32[512,256]{0,1:T(8,128)S(1)}, f32[512,256]{0,1:T(8,128)}, u32[]{:S(2)}) copy-start(f32[512,256]{0,1:T(8,128)} %all-reduce.18.cloned.1.call-done) | copy-start | bytes 1572868
  585.1 26.0 %copy-start.6 = (f32[512,256]{0,1:T(8,128)S(1)}, f32[512,256]{0,1:T(8,128)}, u32[]{:S(2)}) copy-start(f32[512,256]{0,1:T(8,128)} %all-reduce.16.cloned.1.call-done) | copy-start | bytes 1572868
  611.0 208.8 %all-reduce.22.cloned.1.call-start = ((), (), s32[]{:S(2)}) async-start(), calls=%async_computation.4 | async-start | bytes 1048576 | tf_op jit(solution)/shard_map/psum | solution.py:13
  725.4 140.9 %all-gather.7.cloned.1.call-start = ((), (), s32[]{:S(2)}) async-start(), calls=%async_computation.9 | async-start | bytes 4456448 | tf_op jit(solution)/shard_map/all_gather | solution.py:47
  822.3 218.4 %all-reduce.24.cloned.1.call-start = ((), (), s32[]{:S(2)}) async-start(), calls=%async_computation.5 | async-start | bytes 1048576 | tf_op jit(solution)/shard_map/psum | solution.py:13
  866.3 63.3 %copy-start.1 = (f32[512,256]{0,1:T(8,128)S(1)}, f32[512,256]{0,1:T(8,128)}, u32[]{:S(2)}) copy-start(f32[512,256]{0,1:T(8,128)} %all-reduce.22.cloned.1.call-done) | copy-start | bytes 1572868
  931.7 207.1 %all-reduce.26.cloned.1.call-start = ((), (), s32[]{:S(2)}) async-start(), calls=%async_computation.6 | async-start | bytes 1048576 | tf_op jit(solution)/shard_map/psum | solution.py:59
  1044.4 209.5 %all-reduce.30.cloned.1.call-start = ((), (), s32[]{:S(2)}) async-start(), calls=%async_computation.10 | async-start | bytes 1048576 | tf_op jit(solution)/shard_map/psum | solution.py:13
  1141.2 294.1 %all-reduce.28.cloned.1.call-start = ((), (), s32[]{:S(2)}) async-start(), calls=%async_computation.7 | async-start | bytes 1048576 | tf_op jit(solution)/shard_map/psum | solution.py:13
  1257.2 64.4 %copy-start.3 = (f32[512,256]{1,0:T(8,128)S(1)}, f32[512,256]{1,0:T(8,128)}, u32[]{:S(2)}) copy-start(f32[512,256]{1,0:T(8,128)} %all-reduce.26.cloned.1.call-done) | copy-start | bytes 1572868
  1298.1 25.9 %copy-start.5 = (f32[512,256]{0,1:T(8,128)S(1)}, f32[512,256]{0,1:T(8,128)}, u32[]{:S(2)}) copy-start(f32[512,256]{0,1:T(8,128)} %all-reduce.24.cloned.1.call-done) | copy-start | bytes 1572868
Sparse Core Ops, SparseCore 0:
  10.5 97.5 all-reduce.13
  110.8 43.7 all-gather.4
  219.8 108.7 all-reduce.15
  331.6 94.1 all-reduce.17
  428.4 112.5 all-reduce.31
  611.2 111.1 all-reduce.19
  725.5 94.1 all-reduce.21
  822.5 43.7 all-gather.6
  931.8 108.8 all-reduce.23
  1044.5 94.1 all-reduce.25
  1141.3 112.5 all-reduce.29
  1324.1 111.1 all-reduce.27
